TPU v7x, 256 devices: a whole 4x4x8 slice. The times are simulated.
256 devices in a mesh: segment: 4 (over x), ctx: 32 (over y, z), tp: 2 (over core).
Axes of the slice: x: 4, y: 4, z: 8, core: 2. Of those that a mesh axis runs over, the one named last changes fastest.
Arguments:
- mamba_input: bfloat16 [4, 4096, 8192], P('segment', 'ctx', 'tp'), may hold values from -13 to 13
- mamba_gate: bfloat16 [4, 4096, 8192], P('segment', 'ctx', 'tp'), may hold values from -6 to 6
- step_size: bfloat16 [4, 4096, 128], P('segment', 'ctx', 'tp'), may hold values from 0 to 2, as said below
- state_maps: bfloat16 [4, 4096, 256], P('segment', 'ctx'), may hold values from -3 to 3
- decay_rate: float32 [128], P('tp'), may hold values from 0.5 to 2
- skip_gain: float32 [128], P('tp'), may hold values from 0.5 to 1.5
- norm_gain: float32 [8192], P('tp'), may hold values from 0.1 to 1.9
- queries: bfloat16 [4, 4096, 8192], P('segment', 'ctx', 'tp'), may hold values from -155 to 154
- keys: bfloat16 [4, 4096, 1024], P('segment', 'ctx', 'tp'), may hold values from -5 to 5
- values: bfloat16 [4, 4096, 1024], P('segment', 'ctx', 'tp'), may hold values from -6 to 6
- source_len: int32 [4], P('segment'), may hold values from 1638 to 3685
Outputs:
- mamba_handed: bfloat16 [4, 4096, 8192], P('segment', 'ctx', 'tp')
- attention_handed: bfloat16 [4, 4096, 8192], P('segment', 'ctx', 'tp')
Inputs may be any that keep to these rules, and one draw needn't show every extreme that they name: `step_size`: positive.
All inputs are finite; a program needn't handle non-finite values.
Results may differ from a plain program's by a relative error of at most 0.0095.
Values may be sent and summed in bfloat16 or wider, within the bound.
A program may use at most 320 MiB of HBM per device.

v0:
```python
import math
import jax
import jax.numpy as jnp
from jax import lax
from jax.sharding import PartitionSpec as P

QUERY_HEADS = 64
KEY_VALUE_HEADS = 8
HEAD_WIDTH = 128
NST = 128
EM = 8192
HP = 64
BLOCK_LEN = 128
precise = lax.Precision.HIGHEST


def from_behind(array, axis, by):
    size = lax.axis_size(axis)
    return lax.ppermute(array, axis, [(i, (i + by) % size) for i in range(size)])


def join_states(earlier, later):
    return (earlier[0] + later[0], jnp.exp(later[0])[..., None, None] * earlier[1] + later[1])


def scan_blocks(mixer_in, step_in, maps_in, speed_collection, skips):
    tok_rows = mixer_in.shape[0]
    head_count = step_in.shape[1]
    block_len = min(BLOCK_LEN, tok_rows)
    blocks = tok_rows // block_len
    step_float = step_in.astype(jnp.float32).reshape(blocks, block_len, head_count)
    log_decay = -speed_collection[None, None, :] * step_float
    cum_log = jnp.cumsum(log_decay, axis=1)
    x_float = mixer_in.astype(jnp.float32).reshape(blocks, block_len, head_count, HP)
    b_float = maps_in[:, :NST].astype(jnp.float32).reshape(blocks, block_len, NST)
    c_float = maps_in[:, NST:].astype(jnp.float32).reshape(blocks, block_len, NST)
    gram = jnp.einsum("cin,cjn->cij", c_float, b_float, precision=precise)
    lower_tri = (jnp.arange(block_len)[:, None] >= jnp.arange(block_len)[None, :])[None, :, :, None]
    differ = cum_log[:, :, None, :] - cum_log[:, None, :, :]
    decay = jnp.where(lower_tri, jnp.exp(jnp.where(lower_tri, differ, 0.0)), 0.0)
    weights = gram[..., None] * decay * step_float[:, None, :, :]
    inner_out = jnp.einsum("cijh,cjhp->cihp", weights, x_float, precision=precise)
    tail_decay = jnp.exp(cum_log[:, -1:, :] - cum_log) * step_float
    block_states = jnp.einsum("cjh,cjn,cjhp->chnp", tail_decay, b_float, x_float, precision=precise)
    block_logs = cum_log[:, -1, :]
    inc_logs, inc_states = lax.associative_scan(join_states, (block_logs, block_states), axis=0)
    entering = jnp.concatenate([jnp.zeros_like(block_states[:1]), inc_states[:-1]], axis=0)
    enter_logs = jnp.concatenate([jnp.zeros_like(block_logs[:1]), inc_logs[:-1]], axis=0)
    outer_out = jnp.exp(cum_log)[..., None] * jnp.einsum(
        "cin,chnp->cihp", c_float, entering, precision=precise
    )
    mixed = inner_out + outer_out + skips[None, None, :, None] * x_float
    cum_block = (cum_log + enter_logs[:, None, :]).reshape(tok_rows, head_count)
    return (mixed.reshape(tok_rows, head_count, HP), inc_states[-1], inc_logs[-1], cum_block)


def on_device(
    mamba_input,
    mamba_gate,
    step_size,
    state_maps,
    decay_rate,
    skip_gain,
    norm_gain,
    queries,
    keys,
    values,
    source_len,
):
    mixer_in = mamba_input[0]
    gate_in = mamba_gate[0]
    step_in = step_size[0]
    maps_in = state_maps[0]
    tok_rows = mixer_in.shape[0]
    ctx_index = lax.axis_index("ctx")
    chan_rows, chan_steps = (
        lax.all_to_all(mixer_in, "ctx", split_axis=1, concat_axis=0, tiled=True),
        lax.all_to_all(step_in, "ctx", split_axis=1, concat_axis=0, tiled=True),
    )
    all_maps = lax.all_gather(maps_in, "ctx", axis=0, tiled=True)
    sub_heads = chan_steps.shape[1]
    rate_sub = lax.dynamic_slice_in_dim(decay_rate, ctx_index * sub_heads, sub_heads)
    skip_sub = lax.dynamic_slice_in_dim(skip_gain, ctx_index * sub_heads, sub_heads)
    chan_out, _, _, _ = scan_blocks(chan_rows, chan_steps, all_maps, rate_sub, skip_sub)
    chan_out = chan_out.reshape(chan_rows.shape[0], sub_heads * HP).astype(jnp.bfloat16)
    raw = lax.all_to_all(chan_out, "ctx", split_axis=0, concat_axis=1, tiled=True)
    gated = raw.astype(jnp.float32) * jax.nn.silu(gate_in.astype(jnp.float32))
    square_sums = lax.psum(jnp.sum(gated * gated, axis=-1), "tp")
    mean_sq = square_sums / EM
    mamba_out = (gated * lax.rsqrt(mean_sq + 1e-05)[:, None] * norm_gain[None, :]).astype(
        jnp.bfloat16
    )
    query_in = queries[0]
    kv_local = keys.shape[2] // HEAD_WIDTH
    group_width = QUERY_HEADS // KEY_VALUE_HEADS
    query_head_rows = query_in.reshape(tok_rows, kv_local, group_width, HEAD_WIDTH)
    source = source_len[0]
    query_pos = ctx_index * tok_rows + jnp.arange(tok_rows, dtype=jnp.int32)
    scale = 1.0 / math.sqrt(HEAD_WIDTH)
    start_max = jnp.full((kv_local, group_width, tok_rows), -1e30, jnp.float32)
    key_piece = lax.all_gather(keys[0], "ctx", axis=0, tiled=True)
    value_piece = lax.all_gather(values[0], "ctx", axis=0, tiled=True)
    piece_rows = key_piece.shape[0]
    key_head_rows = key_piece.reshape(piece_rows, kv_local, HEAD_WIDTH)
    value_head_rows = value_piece.reshape(piece_rows, kv_local, HEAD_WIDTH)
    key_pos = jnp.arange(piece_rows, dtype=jnp.int32)
    visible = (key_pos[None, :] <= query_pos[:, None]) | (key_pos[None, :] < source)
    scores = (
        jnp.einsum(
            "tkgd,skd->kgts", query_head_rows, key_head_rows, preferred_element_type=jnp.float32
        )
        * scale
    )
    scores = jnp.where(visible[None, None], scores, -jnp.inf)
    new_max = jnp.maximum(start_max, jnp.max(scores, axis=-1))
    weights = jnp.exp(scores - new_max[..., None])
    new_total = jnp.sum(weights, axis=-1)
    product = jnp.einsum(
        "kgts,skd->kgtd",
        weights.astype(jnp.bfloat16),
        value_head_rows,
        preferred_element_type=jnp.float32,
    )
    attention_out = (
        (product / new_total[..., None])
        .transpose(2, 0, 1, 3)
        .reshape(tok_rows, kv_local * group_width * HEAD_WIDTH)
        .astype(jnp.bfloat16)
    )
    mamba_next, attention_next = from_behind((mamba_out, attention_out), "segment", 1)
    return (mamba_next[None], attention_next[None])


def solution(mesh):
    placed = (
        P("segment", "ctx", "tp"),
        P("segment", "ctx", "tp"),
        P("segment", "ctx", "tp"),
        P("segment", "ctx", None),
        P("tp"),
        P("tp"),
        P("tp"),
        P("segment", "ctx", "tp"),
        P("segment", "ctx", "tp"),
        P("segment", "ctx", "tp"),
        P("segment"),
    )
    return jax.shard_map(
        on_device,
        mesh=mesh,
        in_specs=placed,
        out_specs=(P("segment", "ctx", "tp"), P("segment", "ctx", "tp")),
        check_vma=False,
    )
```

profile of v0, /device:TPU:32, one launch (start us, length us, event | category | flops | bytes accessed | tf_op | source)
XLA Modules:
  0.0 349.6 jit_solution(2937649183413915487)
XLA Ops:
  7.2 0.7 all-gather.7.cloned.1.call-update
  7.9 11.4 %all-to-all-start = ((bf16[128,32,2]{0,2,1:T(2,128)(2,1)}), bf16[128,32,2]{0,2,1:T(2,128)(2,1)S(1)}, u32[]{:S(2)}, u32[]{:S(2)}) async-start(bf16[128,32,2]{0,2,1:T(2,128)(2,1)} %bitcast.126), calls=%async_computation | async-start | bytes 32768 | tf_op jit(solution)/shard_map/all_to_all | solution.py:78
  19.3 1.7 copy.106
  21.0 0.6 iota_compare_fusion.1
  21.6 0.7 dynamic-slice_negate_fusion
  22.4 2.3 copy.117
  24.7 3.1 all-to-all-done
  27.8 6.7 %all-to-all-start.1 = ((bf16[128,32,128]{0,2,1:T(8,128)(2,1)}), bf16[128,32,128]{0,2,1:T(8,128)(2,1)S(1)}, u32[]{:S(2)}, u32[]{:S(2)}) async-start(bf16[128,32,128]{0,2,1:T(8,128)(2,1)} %bitcast.5), calls=%async_computation.1 | async-start | bytes 2097152 | tf_op jit(solution)/shard_map/all_to_all | solution.py:77
  34.6 2.8 copy.87
  37.4 1.8 fusion.61
  40.1 1.3 copy.94
  41.8 1.9 copy.88
  43.7 1.6 exp.51
  45.7 0.7 copy.100
  46.6 0.6 copy.90
  47.2 3.3 copy.92
  50.9 41.8 %all-gather.7.cloned.1.call-done = bf16[1,4096,256]{2,1,0:T(8,128)(2,1)} async-done(((bf16[1,128,256]{2,1,0:T(8,128)(2,1)}), bf16[1,4096,256]{2,1,0:T(8,128)(2,1)}) %all-gather.7.cloned.1.call-update) | async-done | bytes 2097168 | tf_op jit(solution)/shard_map/all_gather | solution.py:80
  92.7 3.0 fusion.54
  95.7 2.4 fusion.36
  98.1 0.6 slice.166
  98.9 1.0 copy-done.2
  100.0 0.8 copy-done.4
  101.1 0.5 copy-done.5
  101.7 0.7 pad_maximum_fusion.3
  102.3 1.6 pad.34
  103.9 1.5 pad_add_fusion
  105.4 3.4 pad.35
  108.8 1.7 add.123
  110.5 5.1 %pad.37 = f32[8,2,128,64]{2,3,1,0:T(8,128)} pad(f32[4,2,128,64]{2,3,1,0:T(8,128)} %add.123, f32[]{:T(128)} %constant.9.clone.1), padding=1_0_1x0_0_0x0_0_0x0_0_0 | pad | bytes 786436 | tf_op jit(solution)/shard_map/pad | solution.py:46
  115.6 1.1 fusion.46
  116.8 3.2 pad.36
  120.0 2.1 add.125
  122.1 1.4 fusion.45
  123.5 0.8 pad_maximum_fusion.1
  124.3 9.2 %pad.38 = f32[16,2,128,64]{2,3,1,0:T(8,128)} pad(f32[8,2,128,64]{2,3,1,0:T(8,128)} %pad_maximum_fusion.1, f32[]{:T(128)} %constant.9.clone.1), padding=0_1_1x0_0_0x0_0_0x0_0_0 | pad | bytes 1572868 | tf_op jit(solution)/shard_map/pad | solution.py:46
  133.5 9.2 %pad.39 = f32[16,2,128,64]{2,3,1,0:T(8,128)} pad(f32[8,2,128,64]{2,3,1,0:T(8,128)} %add.125, f32[]{:T(128)} %constant.9.clone.1), padding=1_0_1x0_0_0x0_0_0x0_0_0 | pad | bytes 1572868 | tf_op jit(solution)/shard_map/pad | solution.py:46
  142.7 2.7 add.127
  145.5 16.6 %pad.73 = f32[32,2,128,64]{2,3,1,0:T(8,128)} pad(f32[16,2,128,64]{2,3,1,0:T(8,128)} %add.127, f32[]{:T(128)} %constant.9.clone.1), padding=1_0_1x0_0_0x0_0_0x0_0_0 | pad | bytes 3145732
  162.0 1.7 fusion.44
  163.8 1.0 pad_maximum_fusion
  164.8 12.4 %pad.51 = f32[31,2,128,64]{2,3,1,0:T(8,128)S(1)} pad(f32[16,2,128,64]{2,3,1,0:T(8,128)} %pad_maximum_fusion, f32[]{:T(128)} %constant.9.clone.1), padding=0_0_1x0_0_0x0_0_0x0_0_0 | pad | bytes 3080196 | tf_op jit(solution)/shard_map/slice | solution.py:47
  177.2 2.4 fusion.62
  179.7 4.9 %fusion.6 = f32[32,2,128,64]{2,3,1,0:T(8,128)S(1)} fusion(bf16[32,128,2,64]{1,3,2,0:T(8,128)(2,1)S(1)} %bitcast.106, f32[32,128,2]{1,2,0:T(2,128)S(1)} %copy-done.9, f32[32,128,2]{1,2,0:T(2,128)S(1)} %copy-done.8, f32[32,128,128]{2,1,0:T(8,128)S(1)} %fusion.62, pred[128,128]{1,0:T(8,128)(4,1)S(1)} %copy-done.11), kind=kOutput, calls=%fused_computation.7 | convolution fusion | flops 810549248 | bytes 5324800 | tf_op jit(solution)/shard_map/cijh,cjhp->cihp/dot_general | solution.py:42
  184.6 3.3 fusion.15
  187.9 7.1 %all-to-all-start.2 = ((bf16[32,128,128]{1,2,0:T(8,128)(2,1)}), bf16[32,128,128]{1,2,0:T(8,128)(2,1)S(1)}, u32[]{:S(2)}, u32[]{:S(2)}) async-start(bf16[32,128,128]{1,2,0:T(8,128)(2,1)} %bitcast.115), calls=%async_computation.2 | async-start | bytes 2097152 | tf_op jit(solution)/shard_map/all_to_all | solution.py:86
  195.1 0.7 all-gather.11.cloned.1.call-update
  195.8 1.6 copy.121
  198.1 1.4 copy.122
  199.6 2.1 fusion.32
  201.7 17.6 %all-to-all-done.2 = bf16[32,128,128]{1,2,0:T(8,128)(2,1)S(1)} async-done(((bf16[32,128,128]{1,2,0:T(8,128)(2,1)}), bf16[32,128,128]{1,2,0:T(8,128)(2,1)S(1)}, u32[]{:S(2)}, u32[]{:S(2)}) %all-to-all-start.2) | async-done | bytes 1048608 | tf_op jit(solution)/shard_map/all_to_all | solution.py:86
  219.3 1.6 convert_element_type.78
  220.9 2.9 copy.118
  223.8 2.3 fusion.24
  226.2 2.5 psum.7
  228.7 2.6 fusion.31
  231.3 1.5 collective-permute-start
  232.8 26.4 %fusion.2 = (f32[4,8,128]{2,1,0:T(8,128)S(1)}, f32[4,4096,128,8]{2,1,3,0:T(8,128)}) fusion(pred[128,4096]{0,1:T(8,128)(4,1)S(1)} %fusion.32, bf16[4096,4,128,1]{0,2,3,1:T(8,128)(2,1)} %bitcast.116, bf16[128,4,8,128]{3,2,1,0:T(8,128)(2,1)S(1)} %bitcast.114), kind=kOutput, calls=%fused_computation.4 | convolution fusion | flops 4345294848 | bytes 72892416 | tf_op jit(solution)/shard_map/tkgd,skd->kgts/dot_general | solution.py:109
  259.3 21.8 %fusion = f32[4,8,128]{2,1,0:T(8,128)S(1)} fusion(f32[4,4096,128,8]{2,1,3,0:T(8,128)} %get-tuple-element.17, f32[4,8,128]{2,1,0:T(8,128)S(1)} %broadcast_maximum_fusion, pred[128,4096]{0,1:T(8,128)(4,1)S(1)} %fusion.32), kind=kLoop, calls=%fused_computation.2 | loop fusion | flops 67104768 | bytes 67665920 | tf_op jit(solution)/shard_map/reduce_sum | solution.py:117
  281.6 6.4 %copy.109 = bf16[1,4096,512]{1,2,0:T(8,128)(2,1)} copy(bf16[1,4096,512]{2,1,0:T(8,128)(2,1)} %all-gather.11.cloned.1.call-done) | data formatting | bytes 8388608 | tf_op jit(solution)/shard_map/all_gather | solution.py:102
  287.9 25.5 %fusion.16 = bf16[128,4,8,128]{0,3,2,1:T(8,128)(2,1)S(1)} fusion(bf16[4096,4,128,1]{0,2,3,1:T(8,128)(2,1)} %bitcast.117, f32[4,4096,128,8]{2,1,3,0:T(8,128)} %get-tuple-element.17, f32[4,8,128]{2,1,0:T(8,128)S(1)} %broadcast_maximum_fusion, pred[128,4096]{0,1:T(8,128)(4,1)S(1)} %fusion.32, f32[128,4,8]{0,2,1:T(8,128)S(1)} %bitcast.127), kind=kOutput, calls=%fused_computation.20 | convolution fusion | flops 4363124736 | bytes 72908800 | tf_op jit(solution)/shard_map/kgts,skd->kgtd/dot_general | solution.py:118
  313.9 1.5 collective-permute-start.1
  315.4 24.3 %collective-permute-done.1 = bf16[128,4096]{1,0:T(8,128)(2,1)S(1)} collective-permute-done((bf16[128,4096]{1,0:T(8,128)(2,1)S(1)}, bf16[128,4096]{1,0:T(8,128)(2,1)S(1)}, u32[]{:S(2)}, u32[]{:S(2)}) %collective-permute-start.1) | collective-permute-done | bytes 1048608 | tf_op jit(solution)/shard_map/ppermute | solution.py:19
  339.8 2.3 copy.133
  342.1 1.0 copy.134
  (80 shorter events, 4.2 us)
Async XLA Ops:
  7.2 17.5 %copy-start.12 = (f32[64]{0:T(128)S(1)}, f32[64]{0:T(128)}, u32[]{:S(2)}) copy-start(f32[64]{0:T(128)} %param.16) | copy-start | bytes 772
  7.2 85.5 %all-gather.7.cloned.1.call-start = ((), (), s32[]{:S(2)}) async-start(), calls=%async_computation.3 | async-start | bytes 2162688 | tf_op jit(solution)/shard_map/all_gather | solution.py:80
  7.9 19.9 %all-to-all-start = ((bf16[128,32,2]{0,2,1:T(2,128)(2,1)}), bf16[128,32,2]{0,2,1:T(2,128)(2,1)S(1)}, u32[]{:S(2)}, u32[]{:S(2)}) async-start(bf16[128,32,2]{0,2,1:T(2,128)(2,1)} %bitcast.126), calls=%async_computation | async-start | bytes 32768 | tf_op jit(solution)/shard_map/all_to_all | solution.py:78
  19.3 213.5 %all-gather.9.cloned.1.call-start = ((), (), s32[]{:S(2)}) async-start(), calls=%async_computation.4 | async-start | bytes 4325376 | tf_op jit(solution)/shard_map/all_gather | solution.py:101
  27.8 67.9 %all-to-all-start.1 = ((bf16[128,32,128]{0,2,1:T(8,128)(2,1)}), bf16[128,32,128]{0,2,1:T(8,128)(2,1)S(1)}, u32[]{:S(2)}, u32[]{:S(2)}) async-start(bf16[128,32,128]{0,2,1:T(8,128)(2,1)} %bitcast.5), calls=%async_computation.1 | async-start | bytes 2097152 | tf_op jit(solution)/shard_map/all_to_all | solution.py:77
  98.9 1.0 copy-start.2
  100.0 0.8 copy-start.4
  101.1 0.6 copy-start.5
  101.1 15.7 %slice-start.1 = ((f32[8,2,128,64]{2,3,1,0:T(8,128)}), f32[1,2,128,64]{2,3,1,0:T(8,128)S(1)}, s32[]{:S(2)}) async-start(f32[8,2,128,64]{2,3,1,0:T(8,128)} %copy-done.4), calls=%async_computation.7 | async-start | bytes 131072 | tf_op jit(solution)/shard_map/slice | solution.py:46
  116.8 6.7 %slice-start = ((f32[16,2,128,64]{2,3,1,0:T(8,128)}), f32[1,2,128,64]{2,3,1,0:T(8,128)S(1)}, s32[]{:S(2)}) async-start(f32[16,2,128,64]{2,3,1,0:T(8,128)} %copy-done.2), calls=%async_computation.6 | async-start | bytes 131072 | tf_op jit(solution)/shard_map/slice | solution.py:46
  162.0 1.7 copy-start.6
  177.2 2.4 copy-start.8
  177.2 2.4 copy-start.9
  177.2 2.4 copy-start.11
  179.6 5.0 %copy-start = (f32[32,2,128,64]{2,3,1,0:T(8,128)S(1)}, f32[32,2,128,64]{2,3,1,0:T(8,128)}, u32[]{:S(2)}) copy-start(f32[32,2,128,64]{2,3,1,0:T(8,128)} %pad.73) | copy-start | bytes 6291460
  179.6 5.0 %copy-start.1 = (bf16[4096,128]{1,0:T(8,128)(2,1)S(1)}, bf16[4096,128]{1,0:T(8,128)(2,1)}, u32[]{:S(2)}) copy-start(bf16[4096,128]{1,0:T(8,128)(2,1)} %get-tuple-element.3) | copy-start | bytes 3145732
  179.6 5.0 %copy-start.7 = (f32[32,128,2]{1,2,0:T(2,128)S(1)}, f32[32,128,2]{1,2,0:T(2,128)}, u32[]{:S(2)}) copy-start(f32[32,128,2]{1,2,0:T(2,128)} %copy.92) | copy-start | bytes 98308
  187.9 7.9 %copy-start.3 = (bf16[1,128,4096]{2,1,0:T(8,128)(2,1)S(1)}, bf16[1,128,4096]{2,1,0:T(8,128)(2,1)}, u32[]{:S(2)}) copy-start(bf16[1,128,4096]{2,1,0:T(8,128)(2,1)} %param.12) | copy-start | bytes 3145732
  187.9 31.4 %all-to-all-start.2 = ((bf16[32,128,128]{1,2,0:T(8,128)(2,1)}), bf16[32,128,128]{1,2,0:T(8,128)(2,1)S(1)}, u32[]{:S(2)}, u32[]{:S(2)}) async-start(bf16[32,128,128]{1,2,0:T(8,128)(2,1)} %bitcast.115), calls=%async_computation.2 | async-start | bytes 2097152 | tf_op jit(solution)/shard_map/all_to_all | solution.py:86
  195.1 86.5 %all-gather.11.cloned.1.call-start = ((), (), s32[]{:S(2)}) async-start(), calls=%async_computation.5 | async-start | bytes 4325376 | tf_op jit(solution)/shard_map/all_gather | solution.py:102
  223.8 4.8 %copy-start.10 = (f32[4096]{0:T(1024)S(1)}, f32[4096]{0:T(1024)}, u32[]{:S(2)}) copy-start(f32[4096]{0:T(1024)} %param.17) | copy-start | bytes 49156
  231.3 84.2 %collective-permute-start = (bf16[128,4096]{1,0:T(8,128)(2,1)S(1)}, bf16[128,4096]{1,0:T(8,128)(2,1)}, u32[]{:S(2)}, u32[]{:S(2)}) collective-permute-start(bf16[128,4096]{1,0:T(8,128)(2,1)S(1)} %fusion.31), channel_id=1, source_target_pairs={{0,64},{64,128},{128,192},{192,0},{1,65},{65,129},{129,193},{193,1... | collective-permute-start | bytes 3145736 | tf_op jit(solution)/shard_map/ppermute | solution.py:19
  313.9 25.8 %collective-permute-start.1 = (bf16[128,4096]{1,0:T(8,128)(2,1)S(1)}, bf16[128,4096]{1,0:T(8,128)(2,1)S(1)}, u32[]{:S(2)}, u32[]{:S(2)}) collective-permute-start(bf16[128,4096]{1,0:T(8,128)(2,1)S(1)} %copy.111), channel_id=1, source_target_pairs={{0,64},{64,128},{128,192},{192,0},{1,65},{65,129},{129,193},{193,1... | collective-permute-start | bytes 3145736 | tf_op jit(solution)/shard_map/ppermute | solution.py:19
Sparse Core Ops, SparseCore 0:
  10.6 82.0 all-gather.6
  95.2 81.4 all-gather.8
  198.5 83.0 all-gather.10
where the time goes:
time: 356 us; the launch traced here: 350 us
  local copies, waits for them, and re-layouts  101 us (28%)
  waiting for transfers between devices  88.7 us (25%)
  matrix products  64.9 us (18%)
  other arithmetic  49.3 us (14%)
  starting transfers between devices  28.3 us (8%)
  between operations  14.7 us (4%)
    all_gather x1, waiting for transfers between devices, on_device(): all_maps = lax.all_gather(maps_in, 'ctx', axis=0, tiled=True)  41.8 us
    pad x6, local copies, waits for them, and re-layouts, scan_blocks(): lax.associative_scan(join_states, (block_logs, block_states), axis=0)  31.7 us
    dot_general x1, matrix products, on_device(): jnp.einsum('tkgd,skd->kgts', query_head_rows, key_head_rows, preferred_el...  26.4 us
    dot_general x1, matrix products, on_device(): jnp.einsum('kgts,skd->kgtd', weights.astype(jnp.bfloat16), value_head_row...  25.5 us
    unnamed x31, local copies, waits for them, and re-layouts  25.3 us
    ppermute x2, waiting for transfers between devices, from_behind(): lax.ppermute(array, axis, [(i, (i + by) % size) for i in range(size)])  24.3 us
    reduce_sum x1, other arithmetic, on_device(): new_total = jnp.sum(weights, axis=-1)  21.8 us
    all_to_all x1, waiting for transfers between devices, on_device(): lax.all_to_all(chan_out, 'ctx', split_axis=0, concat_axis=1, tiled=True)  17.6 us
  transfers between devices with their start and end apart: 8, of which 5 were waited for; matrix products, arithmetic and copies ran while one was open for 60% of the time, Pallas kernels for 0%

commit v1 on v0

--- a/solution.py
+++ b/solution.py
@@ -77,7 +77,9 @@
         lax.all_to_all(mixer_in, "ctx", split_axis=1, concat_axis=0, tiled=True),
         lax.all_to_all(step_in, "ctx", split_axis=1, concat_axis=0, tiled=True),
     )
-    all_maps = lax.all_gather(maps_in, "ctx", axis=0, tiled=True)
+    all_maps = jnp.concatenate(
+        lax.all_to_all(jnp.stack([maps_in] * lax.axis_size("ctx")), "ctx", 0, 0), axis=0
+    )
     sub_heads = chan_steps.shape[1]
     rate_sub = lax.dynamic_slice_in_dim(decay_rate, ctx_index * sub_heads, sub_heads)
     skip_sub = lax.dynamic_slice_in_dim(skip_gain, ctx_index * sub_heads, sub_heads)

time: 356 us -> 387 us (1.087)
  blocking collectives: 2.46 us -> 22.4 us
  waiting for transfers between devices: 88.7 us -> 108 us
  starting transfers between devices: 28.3 us -> 20.2 us
    all_gather x1 -> x0, waiting for transfers between devices: 41.8 us -> none  [on_device(): all_maps = lax.all_gather(maps_in, 'ctx', axis=0, tiled=True)]
    all_to_all x1, waiting for transfers between devices: 3.13 us -> 44.3 us  [on_device(): lax.all_to_all(jnp.stack([maps_in] * lax.axis_size('ctx')), 'ctx', 0, 0)]
    all_to_all x0 -> x1, blocking collectives: none -> 19.9 us  [on_device(): lax.all_to_all(step_in, 'ctx', split_axis=1, concat_axis=0, tiled=True)]
    all_to_all x1, waiting for transfers between devices: 0.01 us -> 19.1 us  [on_device(): lax.all_to_all(mixer_in, 'ctx', split_axis=1, concat_axis=0, tiled=True)]
    all_to_all x1, starting transfers between devices: 11.4 us -> 5.88 us  [on_device(): lax.all_to_all(jnp.stack([maps_in] * lax.axis_size('ctx')), 'ctx', 0, 0)]
    unnamed x31 -> x37, local copies, waits for them, and re-layouts: 25.3 us -> 24.4 us
  transfers between devices with their start and end apart: 8 -> 7, of which waited for: 5 -> 4; matrix products, arithmetic and copies ran while one was open for 60% -> 54% of each run, Pallas kernels for 0% -> 0%
where the time goes in v1:
time: 387 us; the launch traced here: 381 us
  waiting for transfers between devices  108 us (28%)
  local copies, waits for them, and re-layouts  102 us (26%)
  matrix products  65 us (17%)
  other arithmetic  48.5 us (13%)
  blocking collectives  22.4 us (6%)
  starting transfers between devices  20.2 us (5%)
  between operations  15.1 us (4%)
    all_to_all x1, waiting for transfers between devices, on_device(): lax.all_to_all(jnp.stack([maps_in] * lax.axis_size('ctx')), 'ctx', 0, 0)  44.3 us
    pad x6, local copies, waits for them, and re-layouts, scan_blocks(): lax.associative_scan(join_states, (block_logs, block_states), axis=0)  31.7 us
    dot_general x1, matrix products, on_device(): jnp.einsum('tkgd,skd->kgts', query_head_rows, key_head_rows, preferred_el...  26.5 us
    dot_general x1, matrix products, on_device(): jnp.einsum('kgts,skd->kgtd', weights.astype(jnp.bfloat16), value_head_row...  25.5 us
    ppermute x2, waiting for transfers between devices, from_behind(): lax.ppermute(array, axis, [(i, (i + by) % size) for i in range(size)])  24.9 us
    unnamed x37, local copies, waits for them, and re-layouts  24.4 us
    reduce_sum x1, other arithmetic, on_device(): new_total = jnp.sum(weights, axis=-1)  21.8 us
    all_to_all x1, blocking collectives, on_device(): lax.all_to_all(step_in, 'ctx', split_axis=1, concat_axis=0, tiled=True)  19.9 us
  transfers between devices with their start and end apart: 7, of which 4 were waited for; matrix products, arithmetic and copies ran while one was open for 54% of the time, Pallas kernels for 0%

profile of v1, /device:TPU:32, one launch (start us, length us, event | category | flops | bytes accessed | tf_op | source)
XLA Modules:
  0.0 380.6 jit_solution(18279140901157743070)
XLA Ops:
  7.2 19.9 %all_to_all.44 = bf16[128,32,2]{0,2,1:T(2,128)(2,1)S(1)} all-to-all(bf16[128,32,2]{0,2,1:T(2,128)(2,1)} %bitcast.128), channel_id=1, replica_groups=mesh['segment'=4,'ctx'=32,'tp'=2] {'ctx'}, dimensions={1} | all-to-all | bytes 32768 | tf_op jit(solution)/shard_map/all_to_all | solution.py:78
  27.1 2.4 stack.3
  29.5 5.9 %all-to-all-start = ((bf16[32,128,256]{2,1,0:T(8,128)(2,1)}), bf16[32,128,256]{2,1,0:T(8,128)(2,1)}, u32[]{:S(2)}, u32[]{:S(2)}) async-start(bf16[32,128,256]{2,1,0:T(8,128)(2,1)} %stack.3), calls=%async_computation | async-start | bytes 4194304 | tf_op jit(solution)/shard_map/all_to_all | solution.py:81
  35.4 0.8 copy.106
  36.2 1.3 copy.117
  37.7 0.6 iota_compare_fusion.1
  38.4 2.9 copy.87
  41.3 1.8 fusion.61
  43.7 44.3 %all-to-all-done = bf16[32,128,256]{2,1,0:T(8,128)(2,1)} async-done(((bf16[32,128,256]{2,1,0:T(8,128)(2,1)}), bf16[32,128,256]{2,1,0:T(8,128)(2,1)}, u32[]{:S(2)}, u32[]{:S(2)}) %all-to-all-start) | async-done | bytes 2097184 | tf_op jit(solution)/shard_map/all_to_all | solution.py:81
  88.0 6.2 %all-to-all-start.2 = ((bf16[128,32,128]{0,2,1:T(8,128)(2,1)}), bf16[128,32,128]{0,2,1:T(8,128)(2,1)S(1)}, u32[]{:S(2)}, u32[]{:S(2)}) async-start(bf16[128,32,128]{0,2,1:T(8,128)(2,1)} %bitcast.119), calls=%async_computation.2 | async-start | bytes 2097152 | tf_op jit(solution)/shard_map/all_to_all | solution.py:77
  94.4 1.3 copy.94
  96.1 1.9 copy.88
  98.0 1.6 exp.51
  100.0 0.7 copy.100
  100.9 0.6 copy.90
  101.5 3.3 copy.92
  105.2 3.0 fusion.54
  108.2 19.1 %all-to-all-done.2 = bf16[128,32,128]{0,2,1:T(8,128)(2,1)S(1)} async-done(((bf16[128,32,128]{0,2,1:T(8,128)(2,1)}), bf16[128,32,128]{0,2,1:T(8,128)(2,1)S(1)}, u32[]{:S(2)}, u32[]{:S(2)}) %all-to-all-start.2) | async-done | bytes 1048608 | tf_op jit(solution)/shard_map/all_to_all | solution.py:77
  127.3 2.4 fusion.36
  129.7 0.6 slice.166
  130.6 1.0 copy-done.2
  131.7 0.8 copy-done.4
  132.8 0.5 copy-done.6
  133.3 0.7 pad_maximum_fusion.3
  134.0 1.6 pad.34
  135.6 1.5 pad_add_fusion
  137.1 3.4 pad.35
  140.5 1.7 add.123
  142.2 5.1 %pad.37 = f32[8,2,128,64]{2,3,1,0:T(8,128)} pad(f32[4,2,128,64]{2,3,1,0:T(8,128)} %add.123, f32[]{:T(128)} %constant.9.clone.1), padding=1_0_1x0_0_0x0_0_0x0_0_0 | pad | bytes 786436 | tf_op jit(solution)/shard_map/pad | solution.py:46
  147.3 1.1 fusion.46
  148.4 3.2 pad.36
  151.7 2.1 add.125
  153.7 1.4 fusion.45
  155.2 0.8 pad_maximum_fusion.1
  156.0 9.2 %pad.38 = f32[16,2,128,64]{2,3,1,0:T(8,128)} pad(f32[8,2,128,64]{2,3,1,0:T(8,128)} %pad_maximum_fusion.1, f32[]{:T(128)} %constant.9.clone.1), padding=0_1_1x0_0_0x0_0_0x0_0_0 | pad | bytes 1572868 | tf_op jit(solution)/shard_map/pad | solution.py:46
  165.2 9.2 %pad.39 = f32[16,2,128,64]{2,3,1,0:T(8,128)} pad(f32[8,2,128,64]{2,3,1,0:T(8,128)} %add.125, f32[]{:T(128)} %constant.9.clone.1), padding=1_0_1x0_0_0x0_0_0x0_0_0 | pad | bytes 1572868 | tf_op jit(solution)/shard_map/pad | solution.py:46
  174.4 2.7 add.127
  177.1 16.5 %pad.73 = f32[32,2,128,64]{2,3,1,0:T(8,128)} pad(f32[16,2,128,64]{2,3,1,0:T(8,128)} %add.127, f32[]{:T(128)} %constant.9.clone.1), padding=1_0_1x0_0_0x0_0_0x0_0_0 | pad | bytes 3145732
  193.6 1.7 fusion.44
  195.3 1.0 pad_maximum_fusion
  196.4 12.4 %pad.51 = f32[31,2,128,64]{2,3,1,0:T(8,128)S(1)} pad(f32[16,2,128,64]{2,3,1,0:T(8,128)} %pad_maximum_fusion, f32[]{:T(128)} %constant.9.clone.1), padding=0_0_1x0_0_0x0_0_0x0_0_0 | pad | bytes 3080196 | tf_op jit(solution)/shard_map/slice | solution.py:47
  208.8 2.4 fusion.62
  211.2 4.9 %fusion.6 = f32[32,2,128,64]{2,3,1,0:T(8,128)S(1)} fusion(bf16[32,128,2,64]{1,3,2,0:T(8,128)(2,1)S(1)} %bitcast.107, f32[32,128,2]{1,2,0:T(2,128)S(1)} %copy-done.11, f32[32,128,2]{1,2,0:T(2,128)S(1)} %copy-done.10, f32[32,128,128]{2,1,0:T(8,128)S(1)} %fusion.62, pred[128,128]{1,0:T(8,128)(4,1)S(1)} %copy-done.13), kind=kOutput, calls=%fused_computation.7 | convolution fusion | flops 810549248 | bytes 5324800 | tf_op jit(solution)/shard_map/cijh,cjhp->cihp/dot_general | solution.py:42
  216.2 3.3 fusion.15
  219.5 5.0 %all-to-all-start.3 = ((bf16[32,128,128]{1,2,0:T(8,128)(2,1)}), bf16[32,128,128]{1,2,0:T(8,128)(2,1)S(1)}, u32[]{:S(2)}, u32[]{:S(2)}) async-start(bf16[32,128,128]{1,2,0:T(8,128)(2,1)} %bitcast.116), calls=%async_computation.3 | async-start | bytes 2097152 | tf_op jit(solution)/shard_map/all_to_all | solution.py:88
  224.6 0.7 all-gather.7.cloned.1.call-update
  225.3 1.6 copy.121
  227.6 1.4 copy.122
  229.1 2.1 fusion.32
  231.2 18.6 %all-to-all-done.3 = bf16[32,128,128]{1,2,0:T(8,128)(2,1)S(1)} async-done(((bf16[32,128,128]{1,2,0:T(8,128)(2,1)}), bf16[32,128,128]{1,2,0:T(8,128)(2,1)S(1)}, u32[]{:S(2)}, u32[]{:S(2)}) %all-to-all-start.3) | async-done | bytes 1048608 | tf_op jit(solution)/shard_map/all_to_all | solution.py:88
  249.8 1.6 convert_element_type.78
  251.4 2.9 copy.118
  254.3 2.4 fusion.24
  256.7 2.5 psum.7
  259.1 2.6 fusion.31
  261.7 1.7 collective-permute-start
  263.4 26.5 %fusion.2 = (f32[4,8,128]{2,1,0:T(8,128)S(1)}, f32[4,4096,128,8]{2,1,3,0:T(8,128)}) fusion(pred[128,4096]{0,1:T(8,128)(4,1)S(1)} %fusion.32, bf16[4096,4,128,1]{0,2,3,1:T(8,128)(2,1)} %bitcast.117, bf16[128,4,8,128]{3,2,1,0:T(8,128)(2,1)S(1)} %bitcast.115), kind=kOutput, calls=%fused_computation.4 | convolution fusion | flops 4345294848 | bytes 72892416 | tf_op jit(solution)/shard_map/tkgd,skd->kgts/dot_general | solution.py:111
  290.0 21.8 %fusion = f32[4,8,128]{2,1,0:T(8,128)S(1)} fusion(f32[4,4096,128,8]{2,1,3,0:T(8,128)} %get-tuple-element.17, f32[4,8,128]{2,1,0:T(8,128)S(1)} %broadcast_maximum_fusion, pred[128,4096]{0,1:T(8,128)(4,1)S(1)} %fusion.32), kind=kLoop, calls=%fused_computation.2 | loop fusion | flops 67104768 | bytes 67665920 | tf_op jit(solution)/shard_map/reduce_sum | solution.py:119
  311.8 6.4 %copy.109 = bf16[1,4096,512]{1,2,0:T(8,128)(2,1)} copy(bf16[1,4096,512]{2,1,0:T(8,128)(2,1)} %all-gather.7.cloned.1.call-done) | data formatting | bytes 8388608 | tf_op jit(solution)/shard_map/all_gather | solution.py:104
  318.2 25.5 %fusion.16 = bf16[128,4,8,128]{0,3,2,1:T(8,128)(2,1)S(1)} fusion(bf16[4096,4,128,1]{0,2,3,1:T(8,128)(2,1)} %bitcast.118, f32[4,4096,128,8]{2,1,3,0:T(8,128)} %get-tuple-element.17, f32[4,8,128]{2,1,0:T(8,128)S(1)} %broadcast_maximum_fusion, pred[128,4096]{0,1:T(8,128)(4,1)S(1)} %fusion.32, f32[128,4,8]{0,2,1:T(8,128)S(1)} %bitcast.129), kind=kOutput, calls=%fused_computation.20 | convolution fusion | flops 4363124736 | bytes 72908800 | tf_op jit(solution)/shard_map/kgts,skd->kgtd/dot_general | solution.py:120
  344.2 1.3 collective-permute-start.1
  345.6 24.9 %collective-permute-done.1 = bf16[128,4096]{1,0:T(8,128)(2,1)S(1)} collective-permute-done((bf16[128,4096]{1,0:T(8,128)(2,1)S(1)}, bf16[128,4096]{1,0:T(8,128)(2,1)S(1)}, u32[]{:S(2)}, u32[]{:S(2)}) %collective-permute-start.1) | collective-permute-done | bytes 1048608 | tf_op jit(solution)/shard_map/ppermute | solution.py:19
  370.5 2.3 copy.133
  372.7 1.0 copy.134
  (85 shorter events, 3.8 us)
Async XLA Ops:
  29.5 6.0 %copy-start.9 = (bf16[1,128,512]{2,1,0:T(8,128)(2,1)S(1)}, bf16[1,128,512]{2,1,0:T(8,128)(2,1)}, u32[]{:S(2)}) copy-start(bf16[1,128,512]{2,1,0:T(8,128)(2,1)} %param.19) | copy-start | bytes 393220
  29.5 6.8 %copy-start.5 = (bf16[1,128,4096]{2,1,0:T(8,128)(2,1)S(1)}, bf16[1,128,4096]{2,1,0:T(8,128)(2,1)}, u32[]{:S(2)}) copy-start(bf16[1,128,4096]{2,1,0:T(8,128)(2,1)} %param.11) | copy-start | bytes 3145732
  29.5 58.5 %all-to-all-start = ((bf16[32,128,256]{2,1,0:T(8,128)(2,1)}), bf16[32,128,256]{2,1,0:T(8,128)(2,1)}, u32[]{:S(2)}, u32[]{:S(2)}) async-start(bf16[32,128,256]{2,1,0:T(8,128)(2,1)} %stack.3), calls=%async_computation | async-start | bytes 4194304 | tf_op jit(solution)/shard_map/all_to_all | solution.py:81
  35.3 2.2 copy-start.14
  35.4 2.3 copy-start.15
  35.4 228.0 %all-gather.5.cloned.1.call-start = ((), (), s32[]{:S(2)}) async-start(), calls=%async_computation.4 | async-start | bytes 4325376 | tf_op jit(solution)/shard_map/all_gather | solution.py:103
  88.0 39.3 %all-to-all-start.2 = ((bf16[128,32,128]{0,2,1:T(8,128)(2,1)}), bf16[128,32,128]{0,2,1:T(8,128)(2,1)S(1)}, u32[]{:S(2)}, u32[]{:S(2)}) async-start(bf16[128,32,128]{0,2,1:T(8,128)(2,1)} %bitcast.119), calls=%async_computation.2 | async-start | bytes 2097152 | tf_op jit(solution)/shard_map/all_to_all | solution.py:77
  130.5 1.0 copy-start.2
  131.6 0.8 copy-start.4
  132.7 0.6 copy-start.6
  132.7 15.7 %slice-start.1 = ((f32[8,2,128,64]{2,3,1,0:T(8,128)}), f32[1,2,128,64]{2,3,1,0:T(8,128)S(1)}, s32[]{:S(2)}) async-start(f32[8,2,128,64]{2,3,1,0:T(8,128)} %copy-done.4), calls=%async_computation.7 | async-start | bytes 131072 | tf_op jit(solution)/shard_map/slice | solution.py:46
  148.4 6.7 %slice-start = ((f32[16,2,128,64]{2,3,1,0:T(8,128)}), f32[1,2,128,64]{2,3,1,0:T(8,128)S(1)}, s32[]{:S(2)}) async-start(f32[16,2,128,64]{2,3,1,0:T(8,128)} %copy-done.2), calls=%async_computation.6 | async-start | bytes 131072 | tf_op jit(solution)/shard_map/slice | solution.py:46
  193.6 1.7 copy-start.7
  208.7 2.4 copy-start.10
  208.7 2.4 copy-start.11
  208.8 2.4 copy-start.13
  211.2 5.0 %copy-start = (f32[32,2,128,64]{2,3,1,0:T(8,128)S(1)}, f32[32,2,128,64]{2,3,1,0:T(8,128)}, u32[]{:S(2)}) copy-start(f32[32,2,128,64]{2,3,1,0:T(8,128)} %pad.73) | copy-start | bytes 6291460
  211.2 5.0 %copy-start.1 = (bf16[4096,128]{1,0:T(8,128)(2,1)S(1)}, bf16[4096,128]{1,0:T(8,128)(2,1)}, u32[]{:S(2)}) copy-start(bf16[4096,128]{1,0:T(8,128)(2,1)} %get-tuple-element.3) | copy-start | bytes 3145732
  211.2 5.0 %copy-start.8 = (f32[32,128,2]{1,2,0:T(2,128)S(1)}, f32[32,128,2]{1,2,0:T(2,128)}, u32[]{:S(2)}) copy-start(f32[32,128,2]{1,2,0:T(2,128)} %copy.92) | copy-start | bytes 98308
  219.5 5.8 %copy-start.3 = (bf16[1,128,4096]{2,1,0:T(8,128)(2,1)S(1)}, bf16[1,128,4096]{2,1,0:T(8,128)(2,1)}, u32[]{:S(2)}) copy-start(bf16[1,128,4096]{2,1,0:T(8,128)(2,1)} %param.12) | copy-start | bytes 3145732
  219.5 30.3 %all-to-all-start.3 = ((bf16[32,128,128]{1,2,0:T(8,128)(2,1)}), bf16[32,128,128]{1,2,0:T(8,128)(2,1)S(1)}, u32[]{:S(2)}, u32[]{:S(2)}) async-start(bf16[32,128,128]{1,2,0:T(8,128)(2,1)} %bitcast.116), calls=%async_computation.3 | async-start | bytes 2097152 | tf_op jit(solution)/shard_map/all_to_all | solution.py:88
  224.5 87.3 %all-gather.7.cloned.1.call-start = ((), (), s32[]{:S(2)}) async-start(), calls=%async_computation.5 | async-start | bytes 4325376 | tf_op jit(solution)/shard_map/all_gather | solution.py:104
  254.3 4.8 %copy-start.12 = (f32[4096]{0:T(1024)S(1)}, f32[4096]{0:T(1024)}, u32[]{:S(2)}) copy-start(f32[4096]{0:T(1024)} %param.17) | copy-start | bytes 49156
  261.7 83.8 %collective-permute-start = (bf16[128,4096]{1,0:T(8,128)(2,1)S(1)}, bf16[128,4096]{1,0:T(8,128)(2,1)}, u32[]{:S(2)}, u32[]{:S(2)}) collective-permute-start(bf16[128,4096]{1,0:T(8,128)(2,1)S(1)} %fusion.31), channel_id=1, source_target_pairs={{0,64},{64,128},{128,192},{192,0},{1,65},{65,129},{129,193},{193,1... | collective-permute-start | bytes 3145736 | tf_op jit(solution)/shard_map/ppermute | solution.py:19
  344.2 26.3 %collective-permute-start.1 = (bf16[128,4096]{1,0:T(8,128)(2,1)S(1)}, bf16[128,4096]{1,0:T(8,128)(2,1)S(1)}, u32[]{:S(2)}, u32[]{:S(2)}) collective-permute-start(bf16[128,4096]{1,0:T(8,128)(2,1)S(1)} %copy.111), channel_id=1, source_target_pairs={{0,64},{64,128},{128,192},{192,0},{1,65},{65,129},{129,193},{193,1... | collective-permute-start | bytes 3145736 | tf_op jit(solution)/shard_map/ppermute | solution.py:19
Sparse Core Ops, SparseCore 0:
  38.7 109.0 all-gather.4
  228.0 83.1 all-gather.6
